TPU v7x, 32 devices: a whole 2x2x4 slice. The times are simulated.
32 devices in a mesh: grp: 2 (over x), seq: 16 (over z, y, core).
Axes of the slice: x: 2, y: 2, z: 4, core: 2. Of those that a mesh axis runs over, the one named last changes fastest.
Arguments:
- inputs: bfloat16 [4096, 4096], P(('grp', 'seq')), parts along dimension 0, may hold values from -6 to 6
- in_weight: bfloat16 [4096, 768], replicated, may hold values from -0.09375 to 0.09375
- filter_taps: float32 [2048, 256], P('seq'), may hold values from -6 to 6
- grad_out: bfloat16 [4096, 256], P(('grp', 'seq')), parts along dimension 0, may hold values from -6 to 6
Outputs:
- grad_inputs: bfloat16 [4096, 4096], P(('grp', 'seq')), parts along dimension 0
- grad_weight: float32 [8192, 768], P(('grp', 'seq')), parts along dimension 0
- grad_taps: float32 [4096, 256], P(('grp', 'seq')), parts along dimension 0
There are 2 independent parts, one for each index of `grp`. A program takes and returns all parts, laid end to end along the dimension named above; an argument that names none is the same for every part. Nothing has to cross between parts.
All inputs are finite; a program needn't handle non-finite values.
Results may differ from a plain program's by a relative error of at most 0.0064.
Values sent between devices are 32-bit elements; how exact they have to be, the bound alone decides.
A program may use at most 128 MiB of HBM per device.

v0:
```python
import math

import jax
import jax.numpy as jnp
from jax import lax
from jax.sharding import PartitionSpec as P

full_precision = lax.Precision.HIGHEST


def phase_table(count_rows, count_cols, modulus, sign):
    first_index = lax.iota(jnp.int32, count_rows)
    second = lax.iota(jnp.int32, count_cols)
    product = jnp.remainder(first_index[:, None] * second[None, :], modulus)
    angles = product.astype(jnp.float32) * (2.0 * math.pi / modulus)
    return (jnp.cos(angles), sign * jnp.sin(angles))


def mix_rows(signal, cosines, sines):
    real_part = signal[:, 0]
    imag_part = signal[:, 1]

    def apply_matrix(matrix, values):
        return jnp.einsum("kn,aenc->aekc", matrix, values, precision=full_precision)

    result_real = apply_matrix(cosines, real_part) - apply_matrix(sines, imag_part)
    result_imag = apply_matrix(cosines, imag_part) + apply_matrix(sines, real_part)
    return jnp.stack([result_real, result_imag], axis=1)


def mix_blocks(signal, cosines, sines):
    real_part = signal[:, 0]
    imag_part = signal[:, 1]

    def apply_matrix(matrix, values):
        return jnp.einsum("kp,aepjc->aekjc", matrix, values, precision=full_precision)

    result_real = apply_matrix(cosines, real_part) - apply_matrix(sines, imag_part)
    result_imag = apply_matrix(cosines, imag_part) + apply_matrix(sines, real_part)
    return jnp.stack([result_real, result_imag], axis=1)


def rotate(signal, cosines, sines):
    real_part = signal[:, 0]
    imag_part = signal[:, 1]
    return jnp.stack(
        [real_part * cosines - imag_part * sines, real_part * sines + imag_part * cosines], axis=1
    )


def row_turn(row_count, frequency, seqlen, sign):
    row_index = lax.iota(jnp.int32, row_count)
    product = jnp.remainder(row_index * frequency, seqlen)
    angles = product.astype(jnp.float32) * (2.0 * math.pi / seqlen)
    return (jnp.cos(angles)[:, None], sign * jnp.sin(angles)[:, None])


def block_turn(seq_count, block_rows, device, seqlen, sign):
    freq_rows = lax.iota(jnp.int32, seq_count)[:, None]
    row_index = device * block_rows + lax.iota(jnp.int32, block_rows)[None, :]
    product = jnp.remainder(freq_rows * row_index, seqlen)
    angles = product.astype(jnp.float32) * (2.0 * math.pi / seqlen)
    return (jnp.cos(angles)[:, :, None], sign * jnp.sin(angles)[:, :, None])


def forward_transform(signal, device, seq_count, seqlen):
    row_count = signal.shape[3]
    table_cos, table_sin = phase_table(row_count, row_count, row_count, -1.0)
    block_rows = row_count // seq_count
    moved_rows = lax.all_to_all(signal, "seq", split_axis=3, concat_axis=3, tiled=True)
    shaped = moved_rows.reshape(signal.shape[:3] + (seq_count, block_rows, signal.shape[4]))
    grid_cos, grid_sin = phase_table(seq_count, seq_count, seq_count, -1.0)
    mixed_blocks = mix_blocks(shaped, grid_cos, grid_sin)
    turn_cos, turn_sin = block_turn(seq_count, block_rows, device, seqlen, -1.0)
    flat_rows = rotate(mixed_blocks, turn_cos, turn_sin).reshape(signal.shape)
    gathered_rows = lax.all_to_all(flat_rows, "seq", split_axis=3, concat_axis=3, tiled=True)
    return mix_rows(gathered_rows, table_cos, table_sin)


def inverse_transform(signal, device, seq_count, seqlen):
    row_count = signal.shape[3]
    table_cos, table_sin = phase_table(row_count, row_count, row_count, 1.0)
    rows_back = mix_rows(signal, table_cos, table_sin)
    block_rows = row_count // seq_count
    turn_cos, turn_sin = row_turn(row_count, device, seqlen, 1.0)
    turned = rotate(rows_back, turn_cos, turn_sin)
    moved_rows = lax.all_to_all(turned, "seq", split_axis=3, concat_axis=3, tiled=True)
    shaped = moved_rows.reshape(signal.shape[:3] + (seq_count, block_rows, signal.shape[4]))
    grid_cos, grid_sin = phase_table(seq_count, seq_count, seq_count, 1.0)
    flat_rows = mix_blocks(shaped, grid_cos, grid_sin).reshape(signal.shape)
    return lax.all_to_all(flat_rows, "seq", split_axis=3, concat_axis=3, tiled=True)


def per_device(inputs, in_weight, filter_taps, grad_out):
    row_count = inputs.shape[0]
    channels = filter_taps.shape[1]
    seq_count = lax.axis_size("seq")
    device = lax.axis_index("seq")
    seqlen = row_count * seq_count
    scaling = 1.0 / math.sqrt(seqlen)
    projected = jnp.dot(inputs, in_weight, preferred_element_type=jnp.float32).astype(jnp.bfloat16)
    query_rows = projected[:, :channels].astype(jnp.float32)
    key_rows = projected[:, channels : 2 * channels].astype(jnp.float32)
    value_rows = projected[:, 2 * channels :].astype(jnp.float32)
    gated_input = key_rows * value_rows
    kernel = filter_taps * scaling
    back_grad = grad_out.astype(jnp.float32) * query_rows
    real_inputs = jnp.stack([kernel, gated_input, back_grad], axis=0)
    positions = device * row_count + lax.iota(jnp.int32, row_count)
    twist_angles = positions.astype(jnp.float32) * (math.pi / seqlen)
    twist_cos = jnp.cos(twist_angles)[:, None]
    twist_sin = jnp.sin(twist_angles)[:, None]
    plain = jnp.stack([real_inputs, jnp.zeros_like(real_inputs)], axis=1)
    twisted = jnp.stack([real_inputs * twist_cos, -real_inputs * twist_sin], axis=1)
    signal = jnp.stack([plain, twisted], axis=2)
    spectrum = forward_transform(signal, device, seq_count, seqlen)
    kernel_real, kernel_imag = (spectrum[0, 0], spectrum[0, 1])
    gated_real, gated_imag = (spectrum[1, 0], spectrum[1, 1])
    back_real, back_imag = (spectrum[2, 0], spectrum[2, 1])
    forward_real = kernel_real * gated_real - kernel_imag * gated_imag
    forward_imag = kernel_real * gated_imag + kernel_imag * gated_real
    adjoint_real = kernel_real * back_real + kernel_imag * back_imag
    adjoint_imag = kernel_real * back_imag - kernel_imag * back_real
    filter_real = back_real * gated_real + back_imag * gated_imag
    filter_imag = back_imag * gated_real - back_real * gated_imag
    packed = jnp.stack(
        [
            jnp.stack([forward_real - adjoint_imag, forward_imag + adjoint_real], axis=0),
            jnp.stack([filter_real, filter_imag], axis=0),
        ],
        axis=0,
    )
    timed_back = inverse_transform(packed, device, seq_count, seqlen)
    plain_back = timed_back[:, :, 0]
    twisted_back = timed_back[:, :, 1]
    result_real = plain_back[:, 0] + twist_cos * twisted_back[:, 0] - twist_sin * twisted_back[:, 1]
    result_imag = plain_back[:, 1] + twist_sin * twisted_back[:, 0] + twist_cos * twisted_back[:, 1]
    inverse_norm = 1.0 / (2.0 * seqlen)
    mixed_rows = result_real[0] * inverse_norm
    back_conv = result_imag[0] * inverse_norm
    grad_taps = result_real[1] * (inverse_norm * scaling)
    grad_proj = jnp.concatenate(
        [grad_out.astype(jnp.float32) * mixed_rows, back_conv * value_rows, back_conv * key_rows],
        axis=1,
    ).astype(jnp.bfloat16)
    grad_inputs = lax.dot_general(
        grad_proj, in_weight, (((1,), (1,)), ((), ())), preferred_element_type=jnp.float32
    ).astype(jnp.bfloat16)
    grad_weight = lax.psum_scatter(
        lax.dot_general(
            inputs, grad_proj, (((0,), (0,)), ((), ())), preferred_element_type=jnp.float32
        )
        * scaling,
        "seq",
        scatter_dimension=0,
        tiled=True,
    )
    return (grad_inputs, grad_weight, grad_taps)


def solution(mesh):
    in_specs = (P(("grp", "seq"), None), P(), P("seq", None), P(("grp", "seq"), None))
    out_specs = (P(("grp", "seq"), None), P(("grp", "seq"), None), P(("grp", "seq"), None))
    return jax.shard_map(
        per_device, mesh=mesh, in_specs=in_specs, out_specs=out_specs, check_vma=False
    )
```

profile of v0, /device:TPU:0, one launch (start us, length us, event | category | flops | bytes accessed | tf_op | source)
XLA Modules:
  0.0 337.4 jit_solution(6479415057780081966)
XLA Ops:
  7.2 1.2 copy-done
  8.4 3.8 %convolution_convert_fusion.1 = bf16[128,768]{1,0:T(8,128)(2,1)S(1)} fusion(bf16[128,4096]{1,0:T(8,128)(2,1)S(1)} %copy-done, bf16[4096,768]{1,0:T(8,128)(2,1)} %param.5), kind=kOutput, calls=%fused_computation.19 | convolution fusion | flops 805404672 | bytes 7536640 | tf_op jit(solution)/shard_map/dot_general | solution.py:101
  12.4 0.5 copy-done.2
  13.1 0.2 pad_maximum_fusion
  13.3 2.4 copy.39
  15.7 7.4 %all-to-all-start = ((f32[3,2,2,128,256]{4,1,0,2,3:T(2,128)}), f32[3,2,2,128,256]{4,1,0,2,3:T(2,128)S(1)}, u32[]{:S(2)}, u32[]{:S(2)}) async-start(f32[3,2,2,128,256]{4,1,0,2,3:T(2,128)} %copy.39), calls=%async_computation | async-start | bytes 3145728 | tf_op jit(solution)/shard_map/all_to_all | solution.py:70
  23.2 31.7 %all-to-all-done = f32[3,2,2,128,256]{4,1,0,2,3:T(2,128)S(1)} async-done(((f32[3,2,2,128,256]{4,1,0,2,3:T(2,128)}), f32[3,2,2,128,256]{4,1,0,2,3:T(2,128)S(1)}, u32[]{:S(2)}, u32[]{:S(2)}) %all-to-all-start) | async-done | bytes 1572896 | tf_op jit(solution)/shard_map/all_to_all | solution.py:70
  54.9 0.3 copy.94
  55.4 1.0 fusion.12
  56.4 1.0 fusion.13
  57.4 1.0 fusion.3
  58.4 1.2 multiply_subtract_fusion
  59.6 0.5 copy.96
  60.1 0.5 copy.97
  60.5 0.2 pad_maximum_fusion.1
  60.7 2.4 copy.45
  63.1 9.1 %all-to-all-start.1 = ((f32[3,2,2,128,256]{4,2,0,1,3:T(2,128)}), f32[3,2,2,128,256]{4,2,0,1,3:T(2,128)S(1)}, u32[]{:S(2)}, u32[]{:S(2)}) async-start(f32[3,2,2,128,256]{4,2,0,1,3:T(2,128)} %copy.45), calls=%async_computation.1 | async-start | bytes 3145728 | tf_op jit(solution)/shard_map/all_to_all | solution.py:76
  72.2 0.2 reduce-scatter.2.cloned.1.call-start
  72.5 31.6 %all-to-all-done.1 = f32[3,2,2,128,256]{4,2,0,1,3:T(2,128)S(1)} async-done(((f32[3,2,2,128,256]{4,2,0,1,3:T(2,128)}), f32[3,2,2,128,256]{4,2,0,1,3:T(2,128)S(1)}, u32[]{:S(2)}, u32[]{:S(2)}) %all-to-all-start.1) | async-done | bytes 1572896 | tf_op jit(solution)/shard_map/all_to_all | solution.py:76
  104.1 1.4 fusion.185
  105.5 1.3 copy.66
  106.8 1.9 fusion.10
  108.7 0.6 copy.67
  109.4 1.0 fusion.6
  110.5 1.0 fusion.1
  111.5 1.0 fusion
  112.9 0.8 fusion.45
  113.7 0.8 fusion.22
  114.5 0.8 convolution_add_fusion.3
  115.3 0.9 subtract_bitcast_fusion
  116.3 0.6 copy.48
  116.9 33.6 %all_to_all.20 = f32[2,2,2,128,256]{4,2,0,1,3:T(2,128)S(1)} all-to-all(f32[2,2,2,128,256]{4,2,0,1,3:T(2,128)S(1)} %copy.48), channel_id=1, replica_groups=mesh['grp'=2,'seq'=16] {'seq'}, dimensions={3} | all-to-all | bytes 2097152 | tf_op jit(solution)/shard_map/all_to_all | solution.py:87
  150.5 0.3 copy.95
  151.0 0.7 fusion.17
  151.7 0.7 fusion.18
  152.4 0.7 fusion.5
  153.2 0.3 copy.101
  153.5 0.7 fusion.4
  154.2 0.3 copy.100
  154.6 0.8 copy.54
  155.4 29.5 %all_to_all.21 = f32[2,2,2,128,256]{4,0,1,2,3:T(2,128)S(1)} all-to-all(f32[2,2,2,128,256]{4,0,1,2,3:T(2,128)S(1)} %copy.54), channel_id=1, replica_groups=mesh['grp'=2,'seq'=16] {'seq'}, dimensions={3} | all-to-all | bytes 2097152 | tf_op jit(solution)/shard_map/all_to_all | solution.py:91
  184.9 0.4 fusion.187
  185.7 0.7 copy-done.3
  186.6 6.3 %multiply_bitcast_fusion = f32[4096,768]{0,1:T(8,128)} fusion(bf16[128,4096]{1,0:T(8,128)(2,1)S(1)} %copy-done, bf16[128,256]{1,0:T(8,128)(2,1)S(1)} %fusion.26, bf16[128,256]{1,0:T(8,128)(2,1)S(1)} %get-tuple-element.15, bf16[128,256]{1,0:T(8,128)(2,1)S(1)} %fusion.25), kind=kOutput, calls=%fused_computation | convolution fusion | flops 809041920 | bytes 13828096 | tf_op jit(solution)/shard_map/dot_general | solution.py:150
  192.9 0.7 fusion.28
  193.6 5.9 %convolution_convert_fusion = bf16[128,4096]{1,0:T(8,128)(2,1)} fusion(bf16[4096,768]{1,0:T(8,128)(2,1)} %param.5, bf16[128,256]{1,0:T(8,128)(2,1)S(1)} %fusion.26, bf16[128,256]{1,0:T(8,128)(2,1)S(1)} %get-tuple-element.15, bf16[128,256]{1,0:T(8,128)(2,1)S(1)} %fusion.25), kind=kOutput, calls=%fused_computation.1 | convolution fusion | flops 806420480 | bytes 7536640 | tf_op jit(solution)/shard_map/dot_general | solution.py:146
  199.5 128.7 %reduce-scatter.2.cloned.1.call-done = f32[256,768]{0,1:T(8,128)} async-done(((f32[4096,768]{0,1:T(8,128)}), f32[256,768]{0,1:T(8,128)}) %reduce-scatter.2.cloned.1.call-update) | async-done | bytes 786448 | tf_op jit(solution)/shard_map/reduce_scatter | solution.py:149
  328.2 2.3 copy.57
  (35 shorter events, 1.8 us)
Async XLA Ops:
  7.2 1.2 copy-start
  8.4 3.8 %copy-start.4 = (bf16[128,256]{1,0:T(8,128)(2,1)S(1)}, bf16[128,256]{1,0:T(8,128)(2,1)}, u32[]{:S(2)}) copy-start(bf16[128,256]{1,0:T(8,128)(2,1)} %param.7) | copy-start | bytes 196612
  8.4 3.8 %copy-start.5 = (f32[128,256]{1,0:T(8,128)S(1)}, f32[128,256]{1,0:T(8,128)}, u32[]{:S(2)}) copy-start(f32[128,256]{1,0:T(8,128)} %param.6) | copy-start | bytes 393220
  12.2 0.7 copy-start.2
  15.7 39.3 %all-to-all-start = ((f32[3,2,2,128,256]{4,1,0,2,3:T(2,128)}), f32[3,2,2,128,256]{4,1,0,2,3:T(2,128)S(1)}, u32[]{:S(2)}, u32[]{:S(2)}) async-start(f32[3,2,2,128,256]{4,1,0,2,3:T(2,128)} %copy.39), calls=%async_computation | async-start | bytes 3145728 | tf_op jit(solution)/shard_map/all_to_all | solution.py:70
  63.1 41.0 %all-to-all-start.1 = ((f32[3,2,2,128,256]{4,2,0,1,3:T(2,128)}), f32[3,2,2,128,256]{4,2,0,1,3:T(2,128)S(1)}, u32[]{:S(2)}, u32[]{:S(2)}) async-start(f32[3,2,2,128,256]{4,2,0,1,3:T(2,128)} %copy.45), calls=%async_computation.1 | async-start | bytes 3145728 | tf_op jit(solution)/shard_map/all_to_all | solution.py:76
  72.2 256.0 %reduce-scatter.2.cloned.1.call-start = ((), (), s32[]{:S(2)}) async-start(), calls=%async_computation.5 | async-start | bytes 13369344 | tf_op jit(solution)/shard_map/reduce_scatter | solution.py:149
  109.4 1.1 copy-start.1
  185.5 0.9 copy-start.3
Sparse Core Ops, SparseCore 0:
  193.1 135.1 reduce-scatter.1
where the time goes:
time: 338 us; the launch traced here: 337 us
  waiting for transfers between devices  192 us (57%)
  blocking collectives  63.1 us (19%)
  matrix products  31.4 us (9%)
  local copies, waits for them, and re-layouts  17.4 us (5%)
  starting transfers between devices  16.7 us (5%)
  between operations  14.5 us (4%)
    reduce_scatter x1, waiting for transfers between devices, per_device(): lax.psum_scatter(lax.dot_general(inputs, grad_proj, (((0,), (0,)), ((), (...  129 us
    all_to_all x1, blocking collectives, inverse_transform(): lax.all_to_all(turned, 'seq', split_axis=3, concat_axis=3, tiled=True)  33.6 us
    all_to_all x1, waiting for transfers between devices, forward_transform(): lax.all_to_all(signal, 'seq', split_axis=3, concat_axis=3, tiled=True)  31.7 us
    all_to_all x1, waiting for transfers between devices, forward_transform(): lax.all_to_all(flat_rows, 'seq', split_axis=3, concat_axis=3, tiled=True)  31.6 us
    all_to_all x1, blocking collectives, inverse_transform(): lax.all_to_all(flat_rows, 'seq', split_axis=3, concat_axis=3, tiled=True)  29.5 us
    all_to_all x1, starting transfers between devices, forward_transform(): lax.all_to_all(flat_rows, 'seq', split_axis=3, concat_axis=3, tiled=True)  9.11 us
    dot_general x8, matrix products, apply_matrix(): return jnp.einsum('kn,aenc->aekc', matrix, values, precision=full_precision)  8.28 us
    all_to_all x1, starting transfers between devices, forward_transform(): lax.all_to_all(signal, 'seq', split_axis=3, concat_axis=3, tiled=True)  7.41 us
  transfers between devices with their start and end apart: 3, of which 3 were waited for; matrix products, arithmetic and copies ran while one was open for 2% of the time, Pallas kernels for 0%

commit v1 on v0

v1 whole, which is shorter than its diff:
```python
import functools
import math

import jax
import jax.numpy as jnp
from jax import lax
from jax.experimental import pallas as pl
from jax.experimental.pallas import tpu as pltpu
from jax.sharding import PartitionSpec as P

GROUP = 16


def round_up(value, step):
    return (value + step - 1) // step * step


def remote(src, dst, send_sem, recv_sem, peer):
    return pltpu.make_async_remote_copy(
        src_ref=src,
        dst_ref=dst,
        send_sem=send_sem,
        recv_sem=recv_sem,
        device_id={"seq": peer},
        device_id_type=pl.DeviceIdType.MESH,
    )


def conv_kernel(
    n, cpd, wide, slim, pairs_ref, back_ref, mixed_ref, rest_ref,
    got_pairs, got_back, made_mixed, made_rest, pad_gated, pad_back,
    send_sems, recv_sems, send_back_sems, recv_back_sems,
):
    me = lax.axis_index("seq")
    rows = pairs_ref.shape[1]

    def slot(ref, index, height):
        return ref.at[pl.ds(pl.multiple_of(index * height, 8), height), :]

    barrier = pltpu.get_barrier_semaphore()

    @pl.loop(1, n)
    def _(o):
        pl.semaphore_signal(
            barrier, inc=1, device_id={"seq": lax.rem(me + o, n)},
            device_id_type=pl.DeviceIdType.MESH,
        )

    pl.semaphore_wait(barrier, n - 1)

    def forth(peer, sender):
        return (
            remote(slot(pairs_ref, peer, wide), slot(got_pairs, sender, wide),
                   send_sems.at[0, peer], recv_sems.at[0, sender], peer),
            remote(slot(back_ref, peer, slim), slot(got_back, n - 1 - sender, slim),
                   send_sems.at[1, peer], recv_sems.at[1, sender], peer),
        )

    def home(peer, sender):
        return (
            remote(slot(made_mixed, peer, slim), slot(mixed_ref, sender, slim),
                   send_back_sems.at[0, peer], recv_back_sems.at[0, sender], peer),
            remote(slot(made_rest, n - 1 - peer, wide), slot(rest_ref, sender, wide),
                   send_back_sems.at[1, peer], recv_back_sems.at[1, sender], peer),
        )

    def exchange_start(plan):
        @pl.loop(1, n)
        def _(o):
            for copy in plan(lax.rem(me + o, n), me):
                copy.start()

    def exchange_wait(plan):
        @pl.loop(1, n)
        def _(o):
            other = lax.rem(me + n - o, n)
            for copy in plan(other, other):
                copy.wait_recv()

    def exchange_sent(plan):
        @pl.loop(1, n)
        def _(o):
            for copy in plan(lax.rem(me + o, n), me):
                copy.wait_send()

    exchange_start(forth)
    slot(got_pairs, me, wide)[...] = slot(pairs_ref, me, wide)[...]
    slot(got_back, n - 1 - me, slim)[...] = slot(back_ref, me, slim)[...]
    pad_gated[pl.ds(0, n), :] = jnp.zeros((n, rows), jnp.float32)
    pad_back[pl.ds(0, n), :] = jnp.zeros((n, rows), jnp.float32)
    exchange_wait(forth)

    lane = lax.broadcasted_iota(jnp.int32, (rows, rows), 1)
    line = lax.broadcasted_iota(jnp.int32, (rows, rows), 0)
    keep = lane >= line
    group = min(GROUP, n)

    def turned(first, index):
        block = got_pairs[pl.ds(index * wide + first, 1), :]
        return pltpu.roll(
            jnp.broadcast_to(block, (rows, rows)), 0, 1, stride=1, stride_axis=0
        )

    def channel(c, carry):
        pad_gated[pl.ds(n, n), :] = got_pairs[pl.ds(cpd + c, n, stride=wide), :]
        pad_back[pl.ds(n, n), :] = got_back[pl.ds(c, n, stride=slim), :]

        def some_lags(q, total):
            matrices = []
            for first in (c, cpd + c):
                if isinstance(q, int):
                    before = jnp.zeros((rows, rows), jnp.float32)
                else:
                    before = turned(first, jnp.maximum(q * group - 1, 0))
                    before = jnp.where(q == 0, 0.0, before)
                parts = []
                for e in range(group):
                    now = turned(first, q * group + e)
                    parts.append(jnp.where(keep, now, before).astype(jnp.bfloat16))
                    before = now
                matrices.append(jnp.concatenate(parts, axis=0))
            table = jnp.concatenate(matrices, axis=1)
            left = jnp.concatenate(
                [
                    jnp.concatenate(
                        [pad[pl.ds(n - q * group - e, n), :] for e in range(group)], axis=1
                    ).astype(jnp.bfloat16)
                    for pad in (pad_gated, pad_back)
                ],
                axis=0,
            )
            return total + jnp.dot(left, table, preferred_element_type=jnp.float32)

        total = jnp.zeros((2 * n, 2 * rows), jnp.float32)
        if n == group:
            total = some_lags(0, total)
        else:
            total = lax.fori_loop(0, n // group, some_lags, total)
        made_mixed[pl.ds(c, n, stride=slim), :] = total[:n, :rows]
        made_rest[pl.ds(c, n, stride=wide), :] = total[n:, :rows]
        made_rest[pl.ds(cpd + c, n, stride=wide), :] = total[n:, rows:]
        return carry

    lax.fori_loop(0, cpd, channel, 0)
    exchange_sent(forth)
    exchange_start(home)
    slot(mixed_ref, me, slim)[...] = slot(made_mixed, me, slim)[...]
    slot(rest_ref, me, wide)[...] = slot(made_rest, n - 1 - me, wide)[...]
    exchange_wait(home)
    exchange_sent(home)


def convolve(filter_taps, gated_input, back_grad, n):
    rows, channels = filter_taps.shape
    cpd = channels // n
    wide, slim = round_up(2 * cpd, 8), round_up(cpd, 8)

    def by_owner(signals, height):
        stacked = jnp.stack([s.T.reshape(n, cpd, rows) for s in signals], axis=1)
        stacked = stacked.reshape(n, len(signals) * cpd, rows)
        stacked = jnp.pad(stacked, ((0, 0), (0, height - stacked.shape[1]), (0, 0)))
        return stacked.reshape(n * height, rows)

    def to_rows(blocks, height, count):
        shaped = blocks.reshape(n, height, rows)[:, : count * cpd].reshape(n, count, cpd, rows)
        return [shaped[:, k].reshape(channels, rows).T for k in range(count)]

    vmem = pl.BlockSpec(memory_space=pltpu.VMEM)
    f32 = jnp.float32
    mixed, rest = pl.pallas_call(
        functools.partial(conv_kernel, n, cpd, wide, slim),
        out_shape=(
            jax.ShapeDtypeStruct((n * slim, rows), f32),
            jax.ShapeDtypeStruct((n * wide, rows), f32),
        ),
        in_specs=[vmem, vmem],
        out_specs=(vmem, vmem),
        scratch_shapes=[
            pltpu.VMEM((n * wide, rows), f32),
            pltpu.VMEM((n * slim, rows), f32),
            pltpu.VMEM((n * slim, rows), f32),
            pltpu.VMEM((n * wide, rows), f32),
            pltpu.VMEM((2 * n, rows), f32),
            pltpu.VMEM((2 * n, rows), f32),
            pltpu.SemaphoreType.DMA((2, n)),
            pltpu.SemaphoreType.DMA((2, n)),
            pltpu.SemaphoreType.DMA((2, n)),
            pltpu.SemaphoreType.DMA((2, n)),
        ],
        compiler_params=pltpu.CompilerParams(collective_id=0, has_side_effects=True),
    )(
        by_owner([filter_taps, gated_input], wide),
        by_owner([jnp.flip(back_grad, axis=0)], slim),
    )
    (mixed_rows,) = to_rows(mixed, slim, 1)
    back_conv, grad_taps = to_rows(rest, wide, 2)
    return mixed_rows, jnp.flip(back_conv, axis=0), jnp.flip(grad_taps, axis=0)


def per_device(inputs, in_weight, filter_taps, grad_out):
    row_count = inputs.shape[0]
    channels = filter_taps.shape[1]
    seq_count = lax.axis_size("seq")
    seqlen = row_count * seq_count
    scaling = 1.0 / math.sqrt(seqlen)
    projected = jnp.dot(inputs, in_weight, preferred_element_type=jnp.float32).astype(jnp.bfloat16)
    query_rows = projected[:, :channels].astype(jnp.float32)
    key_rows = projected[:, channels : 2 * channels].astype(jnp.float32)
    value_rows = projected[:, 2 * channels :].astype(jnp.float32)
    gated_input = key_rows * value_rows
    back_grad = grad_out.astype(jnp.float32) * query_rows
    mixed_rows, back_conv, grad_taps = convolve(filter_taps, gated_input, back_grad, seq_count)
    mixed_rows = mixed_rows * scaling
    back_conv = back_conv * scaling
    grad_taps = grad_taps * scaling
    grad_proj = jnp.concatenate(
        [grad_out.astype(jnp.float32) * mixed_rows, back_conv * value_rows, back_conv * key_rows],
        axis=1,
    ).astype(jnp.bfloat16)
    grad_inputs = lax.dot_general(
        grad_proj, in_weight, (((1,), (1,)), ((), ())), preferred_element_type=jnp.float32
    ).astype(jnp.bfloat16)
    grad_weight = lax.psum_scatter(
        lax.dot_general(
            inputs, grad_proj, (((0,), (0,)), ((), ())), preferred_element_type=jnp.float32
        )
        * scaling,
        "seq",
        scatter_dimension=0,
        tiled=True,
    )
    return (grad_inputs, grad_weight, grad_taps)


def solution(mesh):
    in_specs = (P(("grp", "seq"), None), P(), P("seq", None), P(("grp", "seq"), None))
    out_specs = (P(("grp", "seq"), None), P(("grp", "seq"), None), P(("grp", "seq"), None))
    return jax.shard_map(
        per_device, mesh=mesh, in_specs=in_specs, out_specs=out_specs, check_vma=False
    )
```

time: 338 us -> 207 us (0.61)
  blocking collectives: 63.1 us -> 0 us
  waiting for transfers between devices: 192 us -> 132 us
  Pallas kernels: 0 us -> 33.4 us
  starting transfers between devices: 16.7 us -> 0.04 us
  matrix products: 31.4 us -> 17.6 us
  local copies, waits for them, and re-layouts: 17.4 us -> 7.98 us
    all_to_all x2 -> x0, waiting for transfers between devices: 63.3 us -> none  [the longest x1 31.7 us: forward_transform(): lax.all_to_all(signal, 'seq', split_axis=3, concat_axis=3, tiled=True)]
    all_to_all x2 -> x0, blocking collectives: 63.1 us -> none  [the longest x1 33.6 us: inverse_transform(): lax.all_to_all(turned, 'seq', split_axis=3, concat_axis=3, tiled=True)]
    pallas_call x0 -> x1, Pallas kernels: none -> 33.4 us  [convolve(): pl.pallas_call(functools.partial(conv_kernel, n, cpd, wide, slim), out_sh...]
    all_to_all x2 -> x0, starting transfers between devices: 16.5 us -> none  [the longest x1 9.11 us: forward_transform(): lax.all_to_all(flat_rows, 'seq', split_axis=3, concat_axis=3, tiled=True)]
    dot_general x16 -> x0, matrix products: 15.4 us -> none  [the longest x8 8.28 us: apply_matrix(): return jnp.einsum('kn,aenc->aekc', matrix, values, precision=full_precision)]
    another operation x5 -> x1, local copies, waits for them, and re-layouts: 6.26 us -> 0.73 us  [by_owner(): stacked = jnp.stack([s.T.reshape(n, cpd, rows) for s in signals], axis=1)]
    reduce_scatter x1, waiting for transfers between devices: 129 us -> 132 us  [per_device(): lax.psum_scatter(lax.dot_general(inputs, grad_proj, (((0,), (0,)), ((), (...]
    unnamed x17 -> x6, local copies, waits for them, and re-layouts: 6.95 us -> 5.07 us
  transfers between devices with their start and end apart: 3 -> 1, of which waited for: 3 -> 1; matrix products, arithmetic and copies ran while one was open for 2% -> 3% of each run, Pallas kernels for 0% -> 0%
where the time goes in v1:
time: 207 us; the launch traced here: 206 us
  waiting for transfers between devices  132 us (64%)
  Pallas kernels  33.4 us (16%)
  matrix products  17.6 us (9%)
  between operations  14.1 us (7%)
  local copies, waits for them, and re-layouts  7.98 us (4%)
    reduce_scatter x1, waiting for transfers between devices, per_device(): lax.psum_scatter(lax.dot_general(inputs, grad_proj, (((0,), (0,)), ((), (...  132 us
    pallas_call x1, Pallas kernels, convolve(): pl.pallas_call(functools.partial(conv_kernel, n, cpd, wide, slim), out_sh...  33.4 us
    dot_general x1, matrix products, per_device(): lax.dot_general(inputs, grad_proj, (((0,), (0,)), ((), ())), preferred_el...  6.33 us
    dot_general x1, matrix products, per_device(): lax.dot_general(grad_proj, in_weight, (((1,), (1,)), ((), ())), preferred...  5.93 us
    dot_general x1, matrix products, per_device(): jnp.dot(inputs, in_weight, preferred_element_type=jnp.float32)  5.33 us
    unnamed x6, local copies, waits for them, and re-layouts  5.07 us
  transfers between devices with their start and end apart: 1, of which 1 were waited for; matrix products, arithmetic and copies ran while one was open for 3% of the time, Pallas kernels for 0%

profile of v1, /device:TPU:0, one launch (start us, length us, event | category | flops | bytes accessed | tf_op | source)
XLA Modules:
  0.0 206.2 jit_solution(6851350067055553053)
XLA Ops:
  7.2 0.0 copy-start
  7.2 0.0 reduce-scatter.2.cloned.1.call-start
  7.2 1.0 copy.15
  8.3 1.0 copy.16
  9.3 0.0 copy-done
  9.3 5.3 %convolution_convert_fusion.1 = bf16[128,768]{0,1:T(8,128)(2,1)S(1)} fusion(bf16[128,4096]{1,0:T(8,128)(2,1)S(1)} %copy-done, bf16[4096,768]{1,0:T(8,128)(2,1)} %param.5), kind=kOutput, calls=%fused_computation.2 | convolution fusion | flops 805404672 | bytes 7536640 | tf_op jit(solution)/shard_map/dot_general | solution.py:206
  14.7 0.7 copy.18
  15.4 0.8 rev.10
  16.2 33.4 %shard_map.67 = (f32[256,128]{1,0:T(8,128)}, f32[512,128]{1,0:T(8,128)}) custom-call(f32[512,128]{1,0:T(8,128)} %bitcast.27, f32[256,128]{1,0:T(8,128)} %bitcast.28), custom_call_target="tpu_custom_call" | custom-call | tf_op jit(solution)/shard_map/pallas_call | solution.py:170
  49.6 1.0 fusion.5
  50.6 0.2 rev.11
  50.8 1.0 fusion.2
  51.7 6.3 %multiply_bitcast_fusion = f32[4096,768]{0,1:T(8,128)} fusion(bf16[128,4096]{1,0:T(8,128)(2,1)S(1)} %copy-done, bf16[128,256]{0,1:T(8,128)(2,1)S(1)} %get-tuple-element.14, bf16[128,256]{0,1:T(8,128)(2,1)S(1)} %get-tuple-element.13, bf16[128,256]{0,1:T(8,128)(2,1)S(1)} %get-tuple-element.19), kind=kOutput, calls=%fused_computation | convolution fusion | flops 809041920 | bytes 13828096 | tf_op jit(solution)/shard_map/dot_general | solution.py:224
  58.1 0.0 reduce-scatter.2.cloned.1.call-update
  58.1 0.2 rev.12
  58.3 0.8 copy.22
  59.1 5.9 %convolution_convert_fusion = bf16[128,4096]{1,0:T(8,128)(2,1)} fusion(bf16[4096,768]{1,0:T(8,128)(2,1)} %param.5, bf16[128,256]{0,1:T(8,128)(2,1)S(1)} %get-tuple-element.14, bf16[128,256]{0,1:T(8,128)(2,1)S(1)} %get-tuple-element.13, bf16[128,256]{0,1:T(8,128)(2,1)S(1)} %get-tuple-element.19), kind=kOutput, calls=%fused_computation.1 | convolution fusion | flops 806420480 | bytes 7536640 | tf_op jit(solution)/shard_map/dot_general | solution.py:220
  65.0 132.1 %reduce-scatter.2.cloned.1.call-done = f32[256,768]{0,1:T(8,128)} async-done(((f32[4096,768]{0,1:T(8,128)}), f32[256,768]{0,1:T(8,128)}) %reduce-scatter.2.cloned.1.call-update) | async-done | bytes 786448 | tf_op jit(solution)/shard_map/reduce_scatter | solution.py:223
  197.1 2.3 %copy.21 = f32[256,768]{1,0:T(8,128)} copy(f32[256,768]{0,1:T(8,128)} %reduce-scatter.2.cloned.1.call-done) | data formatting | bytes 1572864
  (3 shorter events, 0.1 us)
Async XLA Ops:
  7.2 2.1 %copy-start = (bf16[128,4096]{1,0:T(8,128)(2,1)S(1)}, bf16[128,4096]{1,0:T(8,128)(2,1)}, u32[]{:S(2)}) copy-start(bf16[128,4096]{1,0:T(8,128)(2,1)} %param.4) | copy-start | bytes 3145732
  7.2 189.9 %reduce-scatter.2.cloned.1.call-start = ((), (), s32[]{:S(2)}) async-start(), calls=%async_computation.1 | async-start | bytes 13369344 | tf_op jit(solution)/shard_map/reduce_scatter | solution.py:223
Sparse Core Ops, SparseCore 0:
  58.2 138.8 reduce-scatter.1

commit v2 on v1

--- a/solution.py
+++ b/solution.py
@@ -9,6 +9,9 @@
 from jax.sharding import PartitionSpec as P
 
 GROUP = 16
+TEAM = 8
+CHIPS = 4
+PARTS = 3
 
 
 def round_up(value, step):
@@ -27,12 +30,14 @@
 
 
 def conv_kernel(
-    n, cpd, wide, slim, pairs_ref, back_ref, mixed_ref, rest_ref,
+    n, cpd, wide, slim, pairs_ref, back_ref, cols_ref, mixed_ref, rest_ref, got_cols,
     got_pairs, got_back, made_mixed, made_rest, pad_gated, pad_back,
-    send_sems, recv_sems, send_back_sems, recv_back_sems,
+    send_sems, recv_sems, send_back_sems, recv_back_sems, send_cols_sems, recv_cols_sems,
 ):
     me = lax.axis_index("seq")
     rows = pairs_ref.shape[1]
+    team = cols_ref.shape[0] // TEAM
+    base, mine = me // TEAM * TEAM, lax.rem(me, TEAM)
 
     def slot(ref, index, height):
         return ref.at[pl.ds(pl.multiple_of(index * height, 8), height), :]
@@ -83,7 +88,18 @@
             for copy in plan(lax.rem(me + o, n), me):
                 copy.wait_send()
 
+    def cols(target, sender, peer):
+        return remote(slot(cols_ref, target, team), slot(got_cols, sender, team),
+                      send_cols_sems.at[target], recv_cols_sems.at[sender], base + peer)
+
     exchange_start(forth)
+
+    @pl.loop(1, TEAM)
+    def _(o):
+        other = lax.rem(mine + o, TEAM)
+        cols(other, mine, other).start()
+
+    slot(got_cols, mine, team)[...] = slot(cols_ref, mine, team)[...]
     slot(got_pairs, me, wide)[...] = slot(pairs_ref, me, wide)[...]
     slot(got_back, n - 1 - me, slim)[...] = slot(back_ref, me, slim)[...]
     pad_gated[pl.ds(0, n), :] = jnp.zeros((n, rows), jnp.float32)
@@ -149,8 +165,14 @@
     exchange_wait(home)
     exchange_sent(home)
 
-
-def convolve(filter_taps, gated_input, back_grad, n):
+    @pl.loop(1, TEAM)
+    def _(o):
+        other = lax.rem(mine + o, TEAM)
+        cols(other, mine, other).wait_send()
+        cols(other, other, other).wait_recv()
+
+
+def convolve(filter_taps, gated_input, back_grad, columns, n):
     rows, channels = filter_taps.shape
     cpd = channels // n
     wide, slim = round_up(2 * cpd, 8), round_up(cpd, 8)
@@ -167,14 +189,15 @@
 
     vmem = pl.BlockSpec(memory_space=pltpu.VMEM)
     f32 = jnp.float32
-    mixed, rest = pl.pallas_call(
+    mixed, rest, got_cols = pl.pallas_call(
         functools.partial(conv_kernel, n, cpd, wide, slim),
         out_shape=(
             jax.ShapeDtypeStruct((n * slim, rows), f32),
             jax.ShapeDtypeStruct((n * wide, rows), f32),
+            jax.ShapeDtypeStruct(columns.shape, f32),
         ),
-        in_specs=[vmem, vmem],
-        out_specs=(vmem, vmem),
+        in_specs=[vmem] * 3,
+        out_specs=(vmem,) * 3,
         scratch_shapes=[
             pltpu.VMEM((n * wide, rows), f32),
             pltpu.VMEM((n * slim, rows), f32),
@@ -186,49 +209,210 @@
             pltpu.SemaphoreType.DMA((2, n)),
             pltpu.SemaphoreType.DMA((2, n)),
             pltpu.SemaphoreType.DMA((2, n)),
+            pltpu.SemaphoreType.DMA((TEAM,)),
+            pltpu.SemaphoreType.DMA((TEAM,)),
         ],
         compiler_params=pltpu.CompilerParams(collective_id=0, has_side_effects=True),
     )(
         by_owner([filter_taps, gated_input], wide),
         by_owner([jnp.flip(back_grad, axis=0)], slim),
+        columns,
     )
     (mixed_rows,) = to_rows(mixed, slim, 1)
     back_conv, grad_taps = to_rows(rest, wide, 2)
-    return mixed_rows, jnp.flip(back_conv, axis=0), jnp.flip(grad_taps, axis=0)
+    return mixed_rows, jnp.flip(back_conv, axis=0), jnp.flip(grad_taps, axis=0), got_cols
+
+
+def weight_kernel(
+    n, scaling, cols_ref, proj_ref, weight_ref, grad_inputs_ref, out_ref,
+    left, proj_all, made, got, weights,
+    send_sems, relay_sems, recv_sems, send_sum_sems, recv_sum_sems, weight_sem,
+):
+    me = lax.axis_index("seq")
+    teams = n // TEAM
+    team, mine = me // TEAM, lax.rem(me, TEAM)
+    base, chip, core = team * TEAM, mine // 2, lax.rem(mine, 2)
+    sibling = chip * 2 + 1 - core
+    depth = cols_ref.shape[0] // TEAM
+    rows, width = proj_ref.shape[0] // PARTS, proj_ref.shape[1]
+    block = depth // teams
+
+    load = pltpu.make_async_copy(weight_ref, weights, weight_sem)
+    load.start()
+    barrier = pltpu.get_barrier_semaphore()
+
+    def greet(device):
+        pl.semaphore_signal(
+            barrier, inc=1, device_id={"seq": device}, device_id_type=pl.DeviceIdType.MESH
+        )
+
+    @pl.loop(1, TEAM)
+    def _(o):
+        greet(base + lax.rem(mine + o, TEAM))
+
+    @pl.loop(1, teams)
+    def _(o):
+        greet(lax.rem(team + o, teams) * TEAM + mine)
+
+    pl.semaphore_wait(barrier, TEAM - 1 + teams - 1)
+
+    def held(part, member):
+        return proj_all.at[pl.ds(pl.multiple_of((part * TEAM + member) * rows, 8), rows), :]
+
+    def own(part):
+        return proj_ref.at[pl.ds(part * rows, rows), :]
+
+    def direct(part, o, sender, peer):
+        return remote(own(part), held(part, sender), send_sems.at[part, o],
+                      recv_sems.at[part, sender], base + peer)
+
+    def relay(part, o, member):
+        return remote(held(part, member), held(part, member), relay_sems.at[part, o],
+                      recv_sems.at[part, member], base + sibling)
+
+    def across(o):
+        return lax.rem(chip + o, CHIPS) * 2 + core
+
+    def sums(part, to_team, from_team, peer):
+        def place(ref, index):
+            start = pl.multiple_of((part * teams + index) * block, 8)
+            return ref.at[pl.ds(start, block), :]
+
+        return remote(place(made, to_team), place(got, from_team),
+                      send_sum_sems.at[part, to_team], recv_sum_sems.at[part, from_team],
+                      peer * TEAM + mine)
+
+    for part in range(PARTS):
+        for o in range(1, CHIPS):
+            direct(part, o, mine, across(o)).start()
+        direct(part, 0, mine, sibling).start()
+        held(part, mine)[...] = own(part)[...]
+
+    for s in range(TEAM):
+        left[:, s * rows : (s + 1) * rows] = cols_ref[s * depth : (s + 1) * depth, :].astype(
+            jnp.bfloat16
+        )
+    load.wait()
+    proj = jnp.concatenate(
+        [own(part)[...].astype(jnp.bfloat16) for part in range(PARTS)], axis=1
+    )
+    tile = min(512, weights.shape[0])
+
+    @pl.loop(0, weights.shape[0] // tile)
+    def _(t):
+        start = pl.multiple_of(t * tile, tile)
+        grad_inputs_ref[:, pl.ds(start, tile)] = lax.dot_general(
+            proj, weights[pl.ds(start, tile), :], (((1,), (1,)), ((), ())),
+            preferred_element_type=jnp.float32,
+        ).astype(jnp.bfloat16)
+
+    for part in range(PARTS):
+        for o in range(1, CHIPS):
+            direct(part, o, across(o), across(o)).wait_recv()
+            relay(part, o, across(o)).start()
+        direct(part, 0, sibling, sibling).wait_recv()
+        for o in range(1, CHIPS):
+            relay(part, o, lax.rem(chip + o, CHIPS) * 2 + 1 - core).wait_recv()
+        right = proj_all[part * TEAM * rows : (part + 1) * TEAM * rows, :].astype(jnp.bfloat16)
+
+        def product(index):
+            lines = left[pl.ds(pl.multiple_of(index * block, 16), block), :]
+            return jnp.dot(lines, right, preferred_element_type=jnp.float32)
+
+        def send_one(o, carry):
+            target = lax.rem(team + o, teams)
+            made[pl.ds(pl.multiple_of((part * teams + target) * block, 8), block), :] = product(
+                target
+            )
+            sums(part, target, team, target).start()
+            return carry
+
+        lax.fori_loop(1, teams, send_one, 0)
+        out_ref[:, part * width : (part + 1) * width] = product(team)
+
+    for part in range(PARTS):
+        span = slice(part * width, (part + 1) * width)
+
+        def add_one(o, carry):
+            other = lax.rem(team + o, teams)
+            sums(part, other, other, other).wait_recv()
+            start = pl.multiple_of((part * teams + other) * block, 8)
+            out_ref[:, span] = out_ref[:, span] + got[pl.ds(start, block), :]
+            return carry
+
+        lax.fori_loop(1, teams, add_one, 0)
+        out_ref[:, span] = out_ref[:, span] * scaling
+
+    for part in range(PARTS):
+        for o in range(1, CHIPS):
+            direct(part, o, mine, across(o)).wait_send()
+            relay(part, o, across(o)).wait_send()
+        direct(part, 0, mine, sibling).wait_send()
+
+        def sent_one(o, carry):
+            target = lax.rem(team + o, teams)
+            sums(part, target, team, target).wait_send()
+            return carry
+
+        lax.fori_loop(1, teams, sent_one, 0)
+
+
+def weight_step(columns, proj, in_weight, scaling, n):
+    depth, rows = columns.shape[0] // TEAM, columns.shape[1]
+    width = proj.shape[1]
+    block = in_weight.shape[0] // n
+    f32 = jnp.float32
+    vmem = pl.BlockSpec(memory_space=pltpu.VMEM)
+    return pl.pallas_call(
+        functools.partial(weight_kernel, n, scaling),
+        out_shape=(
+            jax.ShapeDtypeStruct((rows, in_weight.shape[0]), jnp.bfloat16),
+            jax.ShapeDtypeStruct((block, PARTS * width), f32),
+        ),
+        in_specs=[vmem, vmem, pl.BlockSpec(memory_space=pl.ANY)],
+        out_specs=(vmem, vmem),
+        scratch_shapes=[
+            pltpu.VMEM((depth, TEAM * rows), jnp.bfloat16),
+            pltpu.VMEM((PARTS * TEAM * rows, width), f32),
+            pltpu.VMEM((PARTS * depth, width), f32),
+            pltpu.VMEM((PARTS * depth, width), f32),
+            pltpu.VMEM(in_weight.shape, in_weight.dtype),
+            pltpu.SemaphoreType.DMA((PARTS, CHIPS)),
+            pltpu.SemaphoreType.DMA((PARTS, CHIPS)),
+            pltpu.SemaphoreType.DMA((PARTS, TEAM)),
+            pltpu.SemaphoreType.DMA((PARTS, n // TEAM)),
+            pltpu.SemaphoreType.DMA((PARTS, n // TEAM)),
+            pltpu.SemaphoreType.DMA,
+        ],
+        compiler_params=pltpu.CompilerParams(collective_id=1, has_side_effects=True),
+    )(columns, proj, in_weight)
 
 
 def per_device(inputs, in_weight, filter_taps, grad_out):
-    row_count = inputs.shape[0]
+    row_count, depth = inputs.shape
     channels = filter_taps.shape[1]
     seq_count = lax.axis_size("seq")
     seqlen = row_count * seq_count
     scaling = 1.0 / math.sqrt(seqlen)
+    columns = inputs.T.reshape(seq_count // TEAM, TEAM, depth // seq_count, row_count)
+    columns = columns.transpose(1, 0, 2, 3).reshape(depth, row_count).astype(jnp.float32)
     projected = jnp.dot(inputs, in_weight, preferred_element_type=jnp.float32).astype(jnp.bfloat16)
     query_rows = projected[:, :channels].astype(jnp.float32)
     key_rows = projected[:, channels : 2 * channels].astype(jnp.float32)
     value_rows = projected[:, 2 * channels :].astype(jnp.float32)
     gated_input = key_rows * value_rows
     back_grad = grad_out.astype(jnp.float32) * query_rows
-    mixed_rows, back_conv, grad_taps = convolve(filter_taps, gated_input, back_grad, seq_count)
+    mixed_rows, back_conv, grad_taps, got_cols = convolve(
+        filter_taps, gated_input, back_grad, columns, seq_count
+    )
     mixed_rows = mixed_rows * scaling
     back_conv = back_conv * scaling
     grad_taps = grad_taps * scaling
     grad_proj = jnp.concatenate(
         [grad_out.astype(jnp.float32) * mixed_rows, back_conv * value_rows, back_conv * key_rows],
-        axis=1,
-    ).astype(jnp.bfloat16)
-    grad_inputs = lax.dot_general(
-        grad_proj, in_weight, (((1,), (1,)), ((), ())), preferred_element_type=jnp.float32
-    ).astype(jnp.bfloat16)
-    grad_weight = lax.psum_scatter(
-        lax.dot_general(
-            inputs, grad_proj, (((0,), (0,)), ((), ())), preferred_element_type=jnp.float32
-        )
-        * scaling,
-        "seq",
-        scatter_dimension=0,
-        tiled=True,
-    )
+        axis=0,
+    )
+    grad_inputs, grad_weight = weight_step(got_cols, grad_proj, in_weight, scaling, seq_count)
     return (grad_inputs, grad_weight, grad_taps)
 
 

time: 207 us -> 119 us (0.57)
  waiting for transfers between devices: 132 us -> 0 us
  Pallas kernels: 33.4 us -> 101 us
  matrix products: 17.6 us -> 4.11 us
  between operations: 14.1 us -> 0.78 us
  local copies, waits for them, and re-layouts: 7.98 us -> 11.6 us
    reduce_scatter x1 -> x0, waiting for transfers between devices: 132 us -> none  [per_device(): lax.psum_scatter(lax.dot_general(inputs, grad_proj, (((0,), (0,)), ((), (...]
    pallas_call x0 -> x1, Pallas kernels: none -> 53.2 us  [weight_step(): pl.pallas_call(functools.partial(weight_kernel, n, scaling), out_shape=(j...]
    pallas_call x1, Pallas kernels: 33.4 us -> 47.3 us  [convolve(): pl.pallas_call(functools.partial(conv_kernel, n, cpd, wide, slim), out_sh...]
    dot_general x2 -> x0, matrix products: 12.3 us -> none  [the longest x1 6.33 us: per_device(): lax.dot_general(inputs, grad_proj, (((0,), (0,)), ((), ())), preferred_el...]
    unnamed x6 -> x8, local copies, waits for them, and re-layouts: 5.07 us -> 5.75 us
  transfers between devices with their start and end apart: 1 -> 0, of which waited for: 1 -> 0; matrix products, arithmetic and copies ran while one was open for 3% -> 0% of each run, Pallas kernels for 0% -> 0%
where the time goes in v2:
time: 119 us
  Pallas kernels  101 us (85%)
  local copies, waits for them, and re-layouts  11.6 us (10%)
  matrix products  4.11 us (3%)
  other arithmetic  1.53 us (1%)
    pallas_call x1, Pallas kernels, weight_step(): pl.pallas_call(functools.partial(weight_kernel, n, scaling), out_shape=(j...  53.2 us
    pallas_call x1, Pallas kernels, convolve(): pl.pallas_call(functools.partial(conv_kernel, n, cpd, wide, slim), out_sh...  47.3 us
    unnamed x8, local copies, waits for them, and re-layouts  5.75 us
    dot_general x1, matrix products, per_device(): jnp.dot(inputs, in_weight, preferred_element_type=jnp.float32)  4.11 us

profile of v2, /device:TPU:0, one launch (start us, length us, event | category | flops | bytes accessed | tf_op | source)
XLA Modules:
  0.0 118.5 jit_solution(12978507382275844808)
XLA Ops:
  0.6 0.0 copy-start.1
  0.6 0.0 copy-start
  0.7 1.1 copy.13
  1.7 4.1 %convolution_convert_fusion = bf16[128,768]{1,0:T(8,128)(2,1)S(1)} fusion(bf16[128,4096]{1,0:T(8,128)(2,1)} %param.4, bf16[4096,768]{1,0:T(8,128)(2,1)} %weight_ref.1), kind=kOutput, calls=%fused_computation | convolution fusion | flops 805404672 | bytes 7536640 | tf_op jit(solution)/shard_map/dot_general | solution.py:399
  5.9 0.0 copy-done.1
  5.9 0.1 rev.10
  6.0 0.8 copy.17.back_ref
  6.7 0.1 copy.14
  6.9 0.7 copy.15
  7.6 0.0 copy-done
  7.6 0.3 copy.25
  7.9 1.9 %copy.16 = f32[2,8,256,128]{3,2,0,1:T(8,128)} copy(f32[2,8,256,128]{2,1,0,3:T(8,128)S(1)} %bitcast.32) | data formatting | bytes 4194304 | tf_op jit(solution)/shard_map/convert_element_type | solution.py:398
  9.8 47.3 %shard_map.67 = (f32[256,128]{1,0:T(8,128)}, f32[512,128]{1,0:T(8,128)}, f32[4096,128]{1,0:T(8,128)}) custom-call(f32[512,128]{1,0:T(8,128)} %bitcast.34, f32[256,128]{1,0:T(8,128)} %copy.17.back_ref, f32[4096,128]{1,0:T(8,128)} %bitcast.31), custom_call_target="tpu_custom_call" | custom-call | tf_op jit(solution)/shard_map/pallas_call | solution.py:192
  57.1 1.0 copy.18
  58.1 1.0 fusion.1
  59.1 0.1 copy.22
  59.2 0.1 rev.12
  59.3 0.7 broadcast_multiply_fusion
  60.0 0.1 copy.20
  60.1 0.1 rev.11
  60.2 0.8 pad_maximum_fusion.proj_ref
  61.0 53.2 %shard_map.68 = (bf16[128,4096]{1,0:T(8,128)(2,1)}, f32[256,768]{1,0:T(8,128)}) custom-call(f32[4096,128]{1,0:T(8,128)} %get-tuple-element.8.cols_ref, f32[384,256]{1,0:T(8,128)} %pad_maximum_fusion.proj_ref, bf16[4096,768]{1,0:T(8,128)(2,1)} %weight_ref.1), custom_call_target="tpu_custom_call" | custom-call | tf_op jit(solution)/shard_map/pallas_call | solution.py:366
  114.2 2.3 %copy.28 = bf16[128,4096]{1,0:T(8,128)(2,1)} copy(bf16[128,4096]{1,0:T(8,128)(2,1)} %get-tuple-element.23) | data formatting | bytes 2097152
  116.5 2.1 %copy.29 = f32[256,768]{1,0:T(8,128)} copy(f32[256,768]{1,0:T(8,128)} %get-tuple-element.24) | data formatting | bytes 1572864
  (3 shorter events, 0.1 us)
Async XLA Ops:
  0.6 5.2 %copy-start.1 = (bf16[128,256]{1,0:T(8,128)(2,1)S(1)}, bf16[128,256]{1,0:T(8,128)(2,1)}, u32[]{:S(2)}) copy-start(bf16[128,256]{1,0:T(8,128)(2,1)} %param.7) | copy-start | bytes 196612
  0.6 7.0 %copy-start = (bf16[128,4096]{1,0:T(8,128)(2,1)S(1)}, bf16[128,4096]{1,0:T(8,128)(2,1)}, u32[]{:S(2)}) copy-start(bf16[128,4096]{1,0:T(8,128)(2,1)} %param.4) | copy-start | bytes 3145732

commit v3 on v1

v3 whole, which is shorter than its diff:
```python
import functools
import math

import jax
import jax.numpy as jnp
from jax import lax
from jax.experimental import pallas as pl
from jax.experimental.pallas import tpu as pltpu
from jax.sharding import PartitionSpec as P

GROUP = 16
TEAM = 8
CHIPS = 4
PARTS = 3


def round_up(value, step):
    return (value + step - 1) // step * step


def remote(src, dst, send_sem, recv_sem, peer):
    return pltpu.make_async_remote_copy(
        src_ref=src,
        dst_ref=dst,
        send_sem=send_sem,
        recv_sem=recv_sem,
        device_id={"seq": peer},
        device_id_type=pl.DeviceIdType.MESH,
    )


def fused_kernel(
    n, scaling, x_ref, weight_ref, taps_ref, grad_ref,
    grad_inputs_ref, out_ref, grad_taps_ref,
    send_taps, send_gated, send_back, got_taps, got_gated, got_back,
    made_mixed, made_conv, made_taps, home_mixed, home_conv, home_taps,
    pad_gated, pad_back, send_cols, got_cols, left, key_rows, value_rows,
    proj, proj_all, made, got, weights,
    go_sems, come_sems, back_sems, home_sems, send_cols_sems, recv_cols_sems,
    send_sems, relay_sems, recv_sems, send_sum_sems, recv_sum_sems, weight_sems,
):
    f32, bf16 = jnp.float32, jnp.bfloat16
    me = lax.axis_index("seq")
    rows, depth = x_ref.shape
    channels = taps_ref.shape[1]
    cpd = channels // n
    slim = send_taps.shape[0] // n
    teams = n // TEAM
    team, mine = me // TEAM, lax.rem(me, TEAM)
    base, chip, core = team * TEAM, mine // 2, lax.rem(mine, 2)
    sibling = chip * 2 + 1 - core
    block = depth // n
    share = depth // TEAM
    pieces = weight_sems.shape[0]
    piece = depth // pieces

    def slot(ref, index, height):
        return ref.at[pl.ds(pl.multiple_of(index * height, 8), height), :]

    def load(k):
        span = pl.ds(k * piece, piece)
        return pltpu.make_async_copy(
            weight_ref.at[span, :], weights.at[span, :], weight_sems.at[k]
        )

    for k in range(pieces):
        load(k).start()
    barrier = pltpu.get_barrier_semaphore()

    @pl.loop(1, n)
    def _(o):
        pl.semaphore_signal(
            barrier, inc=1, device_id={"seq": lax.rem(me + o, n)},
            device_id_type=pl.DeviceIdType.MESH,
        )

    def spread(ref, values):
        if slim == cpd:
            ref[...] = values
        else:
            for p in range(n):
                ref[p * slim : p * slim + cpd, :] = values[p * cpd : (p + 1) * cpd, :]

    def gather(ref):
        if slim == cpd:
            return ref[...]
        return jnp.concatenate([ref[p * slim : p * slim + cpd, :] for p in range(n)], axis=0)

    anti = (
        lax.broadcasted_iota(jnp.int32, (rows, rows), 0)
        + lax.broadcasted_iota(jnp.int32, (rows, rows), 1)
        == rows - 1
    ).astype(f32)

    def reverse(values):
        return jnp.dot(
            values, anti, preferred_element_type=f32, precision=lax.Precision.HIGHEST
        )

    spread(send_taps, taps_ref[...].T)
    for g in range(TEAM):
        for h in range(teams):
            first = (h * TEAM + g) * block
            send_cols[g * rows : (g + 1) * rows, h * block : (h + 1) * block] = x_ref[
                :, first : first + block
            ].astype(f32)
    pl.semaphore_wait(barrier, n - 1)

    def forth_taps(peer, sender):
        return (remote(slot(send_taps, peer, slim), slot(got_taps, sender, slim),
                       go_sems.at[0, peer], come_sems.at[0, sender], peer),)

    def forth(peer, sender):
        return (
            remote(slot(send_gated, peer, slim), slot(got_gated, sender, slim),
                   go_sems.at[1, peer], come_sems.at[1, sender], peer),
            remote(slot(send_back, peer, slim), slot(got_back, n - 1 - sender, slim),
                   go_sems.at[2, peer], come_sems.at[2, sender], peer),
        )

    def home(peer, sender):
        return (
            remote(slot(made_mixed, peer, slim), slot(home_mixed, sender, slim),
                   back_sems.at[0, peer], home_sems.at[0, sender], peer),
            remote(slot(made_conv, n - 1 - peer, slim), slot(home_conv, sender, slim),
                   back_sems.at[1, peer], home_sems.at[1, sender], peer),
        )

    def home_last(peer, sender):
        return (remote(slot(made_taps, n - 1 - peer, slim), slot(home_taps, sender, slim),
                       back_sems.at[2, peer], home_sems.at[2, sender], peer),)

    def exchange_start(plan):
        @pl.loop(1, n)
        def _(o):
            for copy in plan(lax.rem(me + o, n), me):
                copy.start()

    def exchange_wait(plan):
        @pl.loop(1, n)
        def _(o):
            other = lax.rem(me + n - o, n)
            for copy in plan(other, other):
                copy.wait_recv()

    def exchange_sent(plan):
        @pl.loop(1, n)
        def _(o):
            for copy in plan(lax.rem(me + o, n), me):
                copy.wait_send()

    def cols(target, sender, peer):
        return remote(slot(send_cols, target, rows), slot(got_cols, sender, rows),
                      send_cols_sems.at[target], recv_cols_sems.at[sender], base + peer)

    def cols_start(other):
        cols(other, mine, other).start()

    exchange_start(forth_taps)
    cols_start(sibling)
    total = jnp.zeros((rows, PARTS * channels), f32)
    for k in range(pieces):
        load(k).wait()
        total = total + jnp.dot(
            x_ref[:, k * piece : (k + 1) * piece], weights[k * piece : (k + 1) * piece, :],
            preferred_element_type=f32,
        )
    total = total.astype(bf16).astype(f32)
    key_rows[...] = total[:, channels : 2 * channels]
    value_rows[...] = total[:, 2 * channels :]
    spread(send_gated, (total[:, channels : 2 * channels] * total[:, 2 * channels :]).T)
    spread(send_back, reverse((grad_ref[...].astype(f32) * total[:, :channels]).T))
    exchange_start(forth)
    for o in range(1, CHIPS):
        cols_start(lax.rem(chip + o, CHIPS) * 2 + core)
        cols_start(lax.rem(chip + o, CHIPS) * 2 + 1 - core)

    slot(got_cols, mine, rows)[...] = slot(send_cols, mine, rows)[...]
    slot(got_taps, me, slim)[...] = slot(send_taps, me, slim)[...]
    slot(got_gated, me, slim)[...] = slot(send_gated, me, slim)[...]
    slot(got_back, n - 1 - me, slim)[...] = slot(send_back, me, slim)[...]
    pad_gated[pl.ds(0, n), :] = jnp.zeros((n, rows), f32)
    pad_back[pl.ds(0, n), :] = jnp.zeros((n, rows), f32)
    exchange_wait(forth_taps)
    exchange_wait(forth)

    lane = lax.broadcasted_iota(jnp.int32, (rows, rows), 1)
    line = lax.broadcasted_iota(jnp.int32, (rows, rows), 0)
    keep = lane >= line
    group = min(GROUP, n)

    def turned(source, c, index):
        row = source[pl.ds(index * slim + c, 1), :]
        return pltpu.roll(
            jnp.broadcast_to(row, (rows, rows)), 0, 1, stride=1, stride_axis=0
        )

    def channel(c, carry):
        pad_gated[pl.ds(n, n), :] = got_gated[pl.ds(c, n, stride=slim), :]
        pad_back[pl.ds(n, n), :] = got_back[pl.ds(c, n, stride=slim), :]

        def some_lags(q, total):
            matrices = []
            for source in (got_taps, got_gated):
                if isinstance(q, int):
                    before = jnp.zeros((rows, rows), f32)
                else:
                    before = turned(source, c, jnp.maximum(q * group - 1, 0))
                    before = jnp.where(q == 0, 0.0, before)
                parts = []
                for e in range(group):
                    now = turned(source, c, q * group + e)
                    parts.append(jnp.where(keep, now, before).astype(bf16))
                    before = now
                matrices.append(jnp.concatenate(parts, axis=0))
            table = jnp.concatenate(matrices, axis=1)
            lines = jnp.concatenate(
                [
                    jnp.concatenate(
                        [pad[pl.ds(n - q * group - e, n), :] for e in range(group)], axis=1
                    ).astype(bf16)
                    for pad in (pad_gated, pad_back)
                ],
                axis=0,
            )
            return total + jnp.dot(lines, table, preferred_element_type=f32)

        sums = jnp.zeros((2 * n, 2 * rows), f32)
        if n == group:
            sums = some_lags(0, sums)
        else:
            sums = lax.fori_loop(0, n // group, some_lags, sums)
        made_mixed[pl.ds(c, n, stride=slim), :] = sums[:n, :rows]
        late = reverse(jnp.concatenate([sums[n:, :rows], sums[n:, rows:]], axis=0))
        made_conv[pl.ds(c, n, stride=slim), :] = late[:n]
        made_taps[pl.ds(c, n, stride=slim), :] = late[n:]
        return carry

    lax.fori_loop(0, cpd, channel, 0)
    exchange_start(home)
    exchange_start(home_last)
    slot(home_mixed, me, slim)[...] = slot(made_mixed, me, slim)[...]
    slot(home_conv, me, slim)[...] = slot(made_conv, n - 1 - me, slim)[...]
    slot(home_taps, me, slim)[...] = slot(made_taps, n - 1 - me, slim)[...]

    def held(part, member):
        return slot(proj_all, part * TEAM + member, rows)

    def own(part):
        return proj.at[pl.ds(part * rows, rows), :]

    def direct(part, o, sender, peer):
        return remote(own(part), held(part, sender), send_sems.at[part, o],
                      recv_sems.at[part, sender], base + peer)

    def relay(part, o, member):
        return remote(held(part, member), held(part, member), relay_sems.at[part, o],
                      recv_sems.at[part, member], base + sibling)

    def across(o):
        return lax.rem(chip + o, CHIPS) * 2 + core

    def sums_copy(part, to_team, from_team, peer):
        return remote(slot(made, part * teams + to_team, block),
                      slot(got, part * teams + from_team, block),
                      send_sum_sems.at[part, to_team], recv_sum_sems.at[part, from_team],
                      peer * TEAM + mine)

    exchange_wait(home)
    conv = gather(home_conv).T * scaling
    mixed = gather(home_mixed).T * scaling
    values = (grad_ref[...].astype(f32) * mixed, conv * value_rows[...], conv * key_rows[...])
    for part in range(PARTS):
        rounded = values[part].astype(bf16).astype(f32)
        own(part)[...] = rounded
        held(part, mine)[...] = rounded
    for part in range(PARTS):
        for o in range(1, CHIPS):
            direct(part, o, mine, across(o)).start()
        direct(part, 0, mine, sibling).start()

    @pl.loop(1, TEAM)
    def _(o):
        other = lax.rem(mine + o, TEAM)
        cols(other, mine, other).wait_send()
        cols(other, other, other).wait_recv()

    for s in range(TEAM):
        left[:, s * rows : (s + 1) * rows] = got_cols[s * rows : (s + 1) * rows, :].T.astype(bf16)
    tile = min(512, depth)

    def grad_inputs_tiles(first, last):
        lines = jnp.concatenate(
            [own(part)[...].astype(bf16) for part in range(PARTS)], axis=1
        )

        @pl.loop(first, last)
        def _(t):
            start = pl.multiple_of(t * tile, tile)
            grad_inputs_ref[:, pl.ds(start, tile)] = lax.dot_general(
                lines, weights[pl.ds(start, tile), :], (((1,), (1,)), ((), ())),
                preferred_element_type=f32,
            ).astype(bf16)

    for part in range(PARTS):
        for o in range(1, CHIPS):
            direct(part, o, across(o), across(o)).wait_recv()
            relay(part, o, across(o)).start()
        direct(part, 0, sibling, sibling).wait_recv()
        for o in range(1, CHIPS):
            relay(part, o, lax.rem(chip + o, CHIPS) * 2 + 1 - core).wait_recv()
        right = proj_all[part * TEAM * rows : (part + 1) * TEAM * rows, :].astype(bf16)

        def product(index):
            lines = left[pl.ds(pl.multiple_of(index * block, 16), block), :]
            return jnp.dot(lines, right, preferred_element_type=f32)

        def send_one(o, carry):
            target = lax.rem(team + o, teams)
            slot(made, part * teams + target, block)[...] = product(target)
            sums_copy(part, target, team, target).start()
            return carry

        lax.fori_loop(1, teams, send_one, 0)
        out_ref[:, part * channels : (part + 1) * channels] = product(team)

    grad_inputs_tiles(0, depth // tile)
    exchange_wait(home_last)
    grad_taps_ref[...] = gather(home_taps).T * scaling

    for part in range(PARTS):
        span = slice(part * channels, (part + 1) * channels)

        def add_one(o, carry):
            other = lax.rem(team + o, teams)
            sums_copy(part, other, other, other).wait_recv()
            out_ref[:, span] = out_ref[:, span] + slot(got, part * teams + other, block)[...]
            return carry

        lax.fori_loop(1, teams, add_one, 0)
        out_ref[:, span] = out_ref[:, span] * scaling

    for plan in (forth_taps, forth, home, home_last):
        exchange_sent(plan)
    for part in range(PARTS):
        for o in range(1, CHIPS):
            direct(part, o, mine, across(o)).wait_send()
            relay(part, o, across(o)).wait_send()
        direct(part, 0, mine, sibling).wait_send()

        def sent_one(o, carry):
            target = lax.rem(team + o, teams)
            sums_copy(part, target, team, target).wait_send()
            return carry

        lax.fori_loop(1, teams, sent_one, 0)


def per_device(inputs, in_weight, filter_taps, grad_out):
    rows, depth = inputs.shape
    channels = filter_taps.shape[1]
    n = lax.axis_size("seq")
    scaling = 1.0 / math.sqrt(rows * n)
    slim = round_up(channels // n, 8)
    share = depth // TEAM
    f32, bf16 = jnp.float32, jnp.bfloat16
    vmem = pl.BlockSpec(memory_space=pltpu.VMEM)
    dma = pltpu.SemaphoreType.DMA
    return pl.pallas_call(
        functools.partial(fused_kernel, n, scaling),
        out_shape=(
            jax.ShapeDtypeStruct((rows, depth), bf16),
            jax.ShapeDtypeStruct((depth // n, PARTS * channels), f32),
            jax.ShapeDtypeStruct((rows, channels), f32),
        ),
        in_specs=[vmem, pl.BlockSpec(memory_space=pl.ANY), vmem, vmem],
        out_specs=(vmem,) * 3,
        scratch_shapes=[pltpu.VMEM((n * slim, rows), f32)] * 12
        + [
            pltpu.VMEM((2 * n, rows), f32),
            pltpu.VMEM((2 * n, rows), f32),
            pltpu.VMEM((TEAM * rows, share), f32),
            pltpu.VMEM((TEAM * rows, share), f32),
            pltpu.VMEM((share, TEAM * rows), bf16),
            pltpu.VMEM((rows, channels), f32),
            pltpu.VMEM((rows, channels), f32),
            pltpu.VMEM((PARTS * rows, channels), f32),
            pltpu.VMEM((PARTS * TEAM * rows, channels), f32),
            pltpu.VMEM((PARTS * share, channels), f32),
            pltpu.VMEM((PARTS * share, channels), f32),
            pltpu.VMEM(in_weight.shape, in_weight.dtype),
            dma((3, n)), dma((3, n)), dma((3, n)), dma((3, n)), dma((TEAM,)), dma((TEAM,)),
            dma((PARTS, CHIPS)), dma((PARTS, CHIPS)), dma((PARTS, TEAM)),
            dma((PARTS, n // TEAM)), dma((PARTS, n // TEAM)), dma((4,)),
        ],
        compiler_params=pltpu.CompilerParams(collective_id=0, has_side_effects=True),
    )(inputs, in_weight, filter_taps, grad_out)


def solution(mesh):
    in_specs = (P(("grp", "seq"), None), P(), P("seq", None), P(("grp", "seq"), None))
    out_specs = (P(("grp", "seq"), None), P(("grp", "seq"), None), P(("grp", "seq"), None))
    return jax.shard_map(
        per_device, mesh=mesh, in_specs=in_specs, out_specs=out_specs, check_vma=False
    )
```

time: 207 us -> 100 us (0.48)
  waiting for transfers between devices: 132 us -> 0 us
  Pallas kernels: 33.4 us -> 92.2 us
  matrix products: 17.6 us -> 0 us
  between operations: 14.1 us -> 0.64 us
    reduce_scatter x1 -> x0, waiting for transfers between devices: 132 us -> none  [per_device(): lax.psum_scatter(lax.dot_general(inputs, grad_proj, (((0,), (0,)), ((), (...]
    pallas_call x1, Pallas kernels: 33.4 us -> 92.2 us  [per_device(): pl.pallas_call(functools.partial(fused_kernel, n, scaling), out_shape=(ja...]
    dot_general x3 -> x0, matrix products: 17.6 us -> none  [the longest x1 6.33 us: per_device(): lax.dot_general(inputs, grad_proj, (((0,), (0,)), ((), ())), preferred_el...]
    unnamed x6 -> x3, local copies, waits for them, and re-layouts: 5.07 us -> 5.92 us
  transfers between devices with their start and end apart: 1 -> 0, of which waited for: 1 -> 0; matrix products, arithmetic and copies ran while one was open for 3% -> 0% of each run, Pallas kernels for 0% -> 0%
where the time goes in v3:
time: 100 us; the launch traced here: 98.8 us
  Pallas kernels  92.2 us (92%)
  local copies, waits for them, and re-layouts  5.92 us (6%)
    pallas_call x1, Pallas kernels, per_device(): pl.pallas_call(functools.partial(fused_kernel, n, scaling), out_shape=(ja...  92.2 us
    unnamed x3, local copies, waits for them, and re-layouts  5.92 us

profile of v3, /device:TPU:0, one launch (start us, length us, event | category | flops | bytes accessed | tf_op | source)
XLA Modules:
  0.0 98.8 jit_solution(17984749791353826891)
XLA Ops:
  0.6 92.2 %shard_map.67 = (bf16[128,4096]{1,0:T(8,128)(2,1)}, f32[256,768]{1,0:T(8,128)}, f32[128,256]{1,0:T(8,128)}) custom-call(bf16[128,4096]{1,0:T(8,128)(2,1)} %x_ref.1, bf16[4096,768]{1,0:T(8,128)(2,1)} %weight_ref.1, f32[128,256]{1,0:T(8,128)} %taps_ref.1, bf16[128,256]{1,0:T(8,128)(2,1)} %grad_ref.1), custom_call_target="tpu_custom_call" | custom-call | tf_op jit(solution)/shard_map/pallas_call | solution.py:369
  92.9 2.3 %copy.10 = bf16[128,4096]{1,0:T(8,128)(2,1)} copy(bf16[128,4096]{1,0:T(8,128)(2,1)} %get-tuple-element.6) | data formatting | bytes 2097152
  95.1 2.1 %copy.11 = f32[256,768]{1,0:T(8,128)} copy(f32[256,768]{1,0:T(8,128)} %get-tuple-element.7) | data formatting | bytes 1572864
  97.2 1.6 %copy.12 = f32[128,256]{1,0:T(8,128)} copy(f32[128,256]{1,0:T(8,128)} %get-tuple-element.8) | data formatting | bytes 262144

commit v4 on v3

--- a/solution.py
+++ b/solution.py
@@ -11,7 +11,7 @@
 GROUP = 16
 TEAM = 8
 CHIPS = 4
-PARTS = 3
+PARTS = 6
 
 
 def round_up(value, step):
@@ -43,6 +43,7 @@
     me = lax.axis_index("seq")
     rows, depth = x_ref.shape
     channels = taps_ref.shape[1]
+    width = 3 * channels // PARTS
     cpd = channels // n
     slim = send_taps.shape[0] // n
     teams = n // TEAM
@@ -157,8 +158,13 @@
         cols(other, mine, other).start()
 
     exchange_start(forth_taps)
+    near = (chip + 1 - 2 * lax.rem(chip, 2)) * 2
+    next_pair = lax.rem(chip + 2, CHIPS) * 2
+    corner = lax.rem(chip + 3 - 2 * lax.rem(chip, 2), CHIPS) * 2
     cols_start(sibling)
-    total = jnp.zeros((rows, PARTS * channels), f32)
+    cols_start(near + core)
+    cols_start(next_pair + core)
+    total = jnp.zeros((rows, 3 * channels), f32)
     for k in range(pieces):
         load(k).wait()
         total = total + jnp.dot(
@@ -171,9 +177,10 @@
     spread(send_gated, (total[:, channels : 2 * channels] * total[:, 2 * channels :]).T)
     spread(send_back, reverse((grad_ref[...].astype(f32) * total[:, :channels]).T))
     exchange_start(forth)
-    for o in range(1, CHIPS):
-        cols_start(lax.rem(chip + o, CHIPS) * 2 + core)
-        cols_start(lax.rem(chip + o, CHIPS) * 2 + 1 - core)
+    cols_start(near + 1 - core)
+    cols_start(next_pair + 1 - core)
+    cols_start(corner + core)
+    cols_start(corner + 1 - core)
 
     slot(got_cols, mine, rows)[...] = slot(send_cols, mine, rows)[...]
     slot(got_taps, me, slim)[...] = slot(send_taps, me, slim)[...]
@@ -238,7 +245,6 @@
 
     lax.fori_loop(0, cpd, channel, 0)
     exchange_start(home)
-    exchange_start(home_last)
     slot(home_mixed, me, slim)[...] = slot(made_mixed, me, slim)[...]
     slot(home_conv, me, slim)[...] = slot(made_conv, n - 1 - me, slim)[...]
     slot(home_taps, me, slim)[...] = slot(made_taps, n - 1 - me, slim)[...]
@@ -269,15 +275,18 @@
     exchange_wait(home)
     conv = gather(home_conv).T * scaling
     mixed = gather(home_mixed).T * scaling
-    values = (grad_ref[...].astype(f32) * mixed, conv * value_rows[...], conv * key_rows[...])
+    values = jnp.concatenate(
+        [grad_ref[...].astype(f32) * mixed, conv * value_rows[...], conv * key_rows[...]], axis=1
+    )
     for part in range(PARTS):
-        rounded = values[part].astype(bf16).astype(f32)
+        rounded = values[:, part * width : (part + 1) * width].astype(bf16).astype(f32)
         own(part)[...] = rounded
         held(part, mine)[...] = rounded
     for part in range(PARTS):
         for o in range(1, CHIPS):
             direct(part, o, mine, across(o)).start()
         direct(part, 0, mine, sibling).start()
+    exchange_start(home_last)
 
     @pl.loop(1, TEAM)
     def _(o):
@@ -322,14 +331,14 @@
             return carry
 
         lax.fori_loop(1, teams, send_one, 0)
-        out_ref[:, part * channels : (part + 1) * channels] = product(team)
+        out_ref[:, part * width : (part + 1) * width] = product(team)
 
     grad_inputs_tiles(0, depth // tile)
     exchange_wait(home_last)
     grad_taps_ref[...] = gather(home_taps).T * scaling
 
     for part in range(PARTS):
-        span = slice(part * channels, (part + 1) * channels)
+        span = slice(part * width, (part + 1) * width)
 
         def add_one(o, carry):
             other = lax.rem(team + o, teams)
@@ -356,6 +365,15 @@
         lax.fori_loop(1, teams, sent_one, 0)
 
 
+def write_kernel(*refs):
+    sems = refs[-1]
+    copies = [pltpu.make_async_copy(refs[k], refs[3 + k], sems.at[k]) for k in range(3)]
+    for copy in copies:
+        copy.start()
+    for copy in copies:
+        copy.wait()
+
+
 def per_device(inputs, in_weight, filter_taps, grad_out):
     rows, depth = inputs.shape
     channels = filter_taps.shape[1]
@@ -363,14 +381,15 @@
     scaling = 1.0 / math.sqrt(rows * n)
     slim = round_up(channels // n, 8)
     share = depth // TEAM
+    width = 3 * channels // PARTS
     f32, bf16 = jnp.float32, jnp.bfloat16
     vmem = pl.BlockSpec(memory_space=pltpu.VMEM)
     dma = pltpu.SemaphoreType.DMA
-    return pl.pallas_call(
+    results = pl.pallas_call(
         functools.partial(fused_kernel, n, scaling),
         out_shape=(
             jax.ShapeDtypeStruct((rows, depth), bf16),
-            jax.ShapeDtypeStruct((depth // n, PARTS * channels), f32),
+            jax.ShapeDtypeStruct((depth // n, 3 * channels), f32),
             jax.ShapeDtypeStruct((rows, channels), f32),
         ),
         in_specs=[vmem, pl.BlockSpec(memory_space=pl.ANY), vmem, vmem],
@@ -384,17 +403,27 @@
             pltpu.VMEM((share, TEAM * rows), bf16),
             pltpu.VMEM((rows, channels), f32),
             pltpu.VMEM((rows, channels), f32),
-            pltpu.VMEM((PARTS * rows, channels), f32),
-            pltpu.VMEM((PARTS * TEAM * rows, channels), f32),
-            pltpu.VMEM((PARTS * share, channels), f32),
-            pltpu.VMEM((PARTS * share, channels), f32),
+            pltpu.VMEM((PARTS * rows, width), f32),
+            pltpu.VMEM((PARTS * TEAM * rows, width), f32),
+            pltpu.VMEM((PARTS * share, width), f32),
+            pltpu.VMEM((PARTS * share, width), f32),
             pltpu.VMEM(in_weight.shape, in_weight.dtype),
             dma((3, n)), dma((3, n)), dma((3, n)), dma((3, n)), dma((TEAM,)), dma((TEAM,)),
             dma((PARTS, CHIPS)), dma((PARTS, CHIPS)), dma((PARTS, TEAM)),
             dma((PARTS, n // TEAM)), dma((PARTS, n // TEAM)), dma((4,)),
         ],
-        compiler_params=pltpu.CompilerParams(collective_id=0, has_side_effects=True),
+        compiler_params=pltpu.CompilerParams(
+            collective_id=0, has_side_effects=True, vmem_limit_bytes=59 << 20
+        ),
     )(inputs, in_weight, filter_taps, grad_out)
+    return pl.pallas_call(
+        write_kernel,
+        out_shape=tuple(jax.ShapeDtypeStruct(r.shape, r.dtype) for r in results),
+        in_specs=[vmem] * 3,
+        out_specs=(pl.BlockSpec(memory_space=pl.ANY),) * 3,
+        scratch_shapes=[dma((3,))],
+        compiler_params=pltpu.CompilerParams(vmem_limit_bytes=8 << 20),
+    )(*results)
 
 
 def solution(mesh):

time: 100 us -> 97.5 us (0.975)
  local copies, waits for them, and re-layouts: 5.92 us -> 3.25 us
  Pallas kernels: 92.2 us -> 93.3 us
    unnamed x3 -> x6, local copies, waits for them, and re-layouts: 5.92 us -> 3.25 us
    pallas_call x0 -> x1, Pallas kernels: none -> 1.28 us  [per_device(): pl.pallas_call(write_kernel, out_shape=tuple((jax.ShapeDtypeStruct(r.shap...]
where the time goes in v4:
time: 97.5 us; the launch traced here: 97.3 us
  Pallas kernels  93.3 us (96%)
  local copies, waits for them, and re-layouts  3.25 us (3%)
    pallas_call x1, Pallas kernels, per_device(): pl.pallas_call(functools.partial(fused_kernel, n, scaling), out_shape=(ja...  92.1 us
    unnamed x6, local copies, waits for them, and re-layouts  3.25 us

profile of v4, /device:TPU:0, one launch (start us, length us, event | category | flops | bytes accessed | tf_op | source)
XLA Modules:
  0.0 97.3 jit_solution(1076557072331610986)
XLA Ops:
  0.6 92.1 %shard_map.67 = (bf16[128,4096]{1,0:T(8,128)(2,1)}, f32[256,768]{1,0:T(8,128)}, f32[128,256]{1,0:T(8,128)}) custom-call(bf16[128,4096]{1,0:T(8,128)(2,1)} %x_ref.1, bf16[4096,768]{1,0:T(8,128)(2,1)} %weight_ref.1, f32[128,256]{1,0:T(8,128)} %taps_ref.1, bf16[128,256]{1,0:T(8,128)(2,1)} %grad_ref.1), custom_call_target="tpu_custom_call" | custom-call | tf_op jit(solution)/shard_map/pallas_call | solution.py:388
  92.7 0.0 copy-start
  92.7 1.2 %copy-done = bf16[128,4096]{1,0:T(8,128)(2,1)S(1)} copy-done((bf16[128,4096]{1,0:T(8,128)(2,1)S(1)}, bf16[128,4096]{1,0:T(8,128)(2,1)}, u32[]{:S(2)}) %copy-start) | copy-done | bytes 1048600
  93.9 0.0 copy-start.1
  93.9 1.1 %copy-done.1 = f32[256,768]{1,0:T(8,128)S(1)} copy-done((f32[256,768]{1,0:T(8,128)S(1)}, f32[256,768]{1,0:T(8,128)}, u32[]{:S(2)}) %copy-start.1) | copy-done | bytes 786456
  95.1 0.0 copy-start.2
  95.1 0.9 copy-done.2
  96.0 1.3 %shard_map.68 = (bf16[128,4096]{1,0:T(8,128)(2,1)}, f32[256,768]{1,0:T(8,128)}, f32[128,256]{1,0:T(8,128)}) custom-call(bf16[128,4096]{1,0:T(8,128)(2,1)S(1)} %copy-done, f32[256,768]{1,0:T(8,128)S(1)} %copy-done.1, f32[128,256]{1,0:T(8,128)S(1)} %copy-done.2), custom_call_target="tpu_custom_call" | custom-call | tf_op jit(solution)/shard_map/pallas_call | solution.py:419
Async XLA Ops:
  92.7 1.2 %copy-start = (bf16[128,4096]{1,0:T(8,128)(2,1)S(1)}, bf16[128,4096]{1,0:T(8,128)(2,1)}, u32[]{:S(2)}) copy-start(bf16[128,4096]{1,0:T(8,128)(2,1)} %get-tuple-element.6.refs_0_) | copy-start | bytes 3145732
  93.9 1.1 %copy-start.1 = (f32[256,768]{1,0:T(8,128)S(1)}, f32[256,768]{1,0:T(8,128)}, u32[]{:S(2)}) copy-start(f32[256,768]{1,0:T(8,128)} %get-tuple-element.7.refs_1_) | copy-start | bytes 2359300
  95.1 0.9 copy-start.2

commit v5 on v4

--- a/solution.py
+++ b/solution.py
@@ -413,7 +413,7 @@
             dma((PARTS, n // TEAM)), dma((PARTS, n // TEAM)), dma((4,)),
         ],
         compiler_params=pltpu.CompilerParams(
-            collective_id=0, has_side_effects=True, vmem_limit_bytes=59 << 20
+            collective_id=0, has_side_effects=True, vmem_limit_bytes=44 << 20
         ),
     )(inputs, in_weight, filter_taps, grad_out)
     return pl.pallas_call(

time: 97.5 us -> 97.9 us (level)
  local copies, waits for them, and re-layouts: 3.25 us -> 5.74 us
  Pallas kernels: 93.3 us -> 91.2 us
    unnamed x6 -> x8, local copies, waits for them, and re-layouts: 3.25 us -> 5.74 us
    pallas_call x1, Pallas kernels: 92.1 us -> 89.9 us  [per_device(): pl.pallas_call(functools.partial(fused_kernel, n, scaling), out_shape=(ja...]
where the time goes in v5:
time: 97.9 us; the launch traced here: 97.6 us
  Pallas kernels  91.2 us (93%)
  local copies, waits for them, and re-layouts  5.74 us (6%)
    pallas_call x1, Pallas kernels, per_device(): pl.pallas_call(functools.partial(fused_kernel, n, scaling), out_shape=(ja...  89.9 us
    unnamed x8, local copies, waits for them, and re-layouts  5.74 us

profile of v5, /device:TPU:0, one launch (start us, length us, event | category | flops | bytes accessed | tf_op | source)
XLA Modules:
  0.0 97.6 jit_solution(12924717121570084391)
XLA Ops:
  0.6 0.0 copy-start
  0.6 2.8 %copy-done = bf16[4096,768]{1,0:T(8,128)(2,1)S(1)} copy-done((bf16[4096,768]{1,0:T(8,128)(2,1)S(1)}, bf16[4096,768]{1,0:T(8,128)(2,1)}, u32[]{:S(2)}) %copy-start) | copy-done | bytes 6291480
  3.4 0.0 copy-start.1
  3.4 1.2 %copy-done.1 = bf16[128,4096]{1,0:T(8,128)(2,1)S(1)} copy-done((bf16[128,4096]{1,0:T(8,128)(2,1)S(1)}, bf16[128,4096]{1,0:T(8,128)(2,1)}, u32[]{:S(2)}) %copy-start.1) | copy-done | bytes 1048600
  4.6 0.0 copy-start.2
  4.6 0.9 copy-done.2
  5.5 0.0 copy-start.3
  5.5 0.8 copy-done.3
  6.4 89.9 %shard_map.67 = (bf16[128,4096]{1,0:T(8,128)(2,1)S(1)}, f32[256,768]{1,0:T(8,128)S(1)}, f32[128,256]{1,0:T(8,128)S(1)}) custom-call(bf16[128,4096]{1,0:T(8,128)(2,1)S(1)} %copy-done.1, bf16[4096,768]{1,0:T(8,128)(2,1)S(1)} %copy-done, f32[128,256]{1,0:T(8,128)S(1)} %copy-done.2, bf16[128,256]{1,0:T(8,128)(2,1)S(1)} %copy-done.3), custom_call_target="tpu_custom_call" | custom-call | tf_op jit(solution)/shard_map/pallas_call | solution.py:388
  96.3 1.3 %shard_map.68 = (bf16[128,4096]{1,0:T(8,128)(2,1)}, f32[256,768]{1,0:T(8,128)}, f32[128,256]{1,0:T(8,128)}) custom-call(bf16[128,4096]{1,0:T(8,128)(2,1)S(1)} %get-tuple-element.6.refs_0_, f32[256,768]{1,0:T(8,128)S(1)} %get-tuple-element.7.refs_1_, f32[128,256]{1,0:T(8,128)S(1)} %get-tuple-element.8.refs_2_), custom_call_target="tpu_custom_call" | custom-call | tf_op jit(solution)/shard_map/pallas_call | solution.py:419
Async XLA Ops:
  0.6 2.8 %copy-start = (bf16[4096,768]{1,0:T(8,128)(2,1)S(1)}, bf16[4096,768]{1,0:T(8,128)(2,1)}, u32[]{:S(2)}) copy-start(bf16[4096,768]{1,0:T(8,128)(2,1)} %weight_ref.1) | copy-start | bytes 18874372
  3.4 1.2 %copy-start.1 = (bf16[128,4096]{1,0:T(8,128)(2,1)S(1)}, bf16[128,4096]{1,0:T(8,128)(2,1)}, u32[]{:S(2)}) copy-start(bf16[128,4096]{1,0:T(8,128)(2,1)} %x_ref.1) | copy-start | bytes 3145732
  4.6 0.9 copy-start.2
  5.5 0.8 copy-start.3
